TPU v7x, 512 devices: a whole 4x4x16 slice. The times are simulated.
512 devices in a mesh: tile: 32 (over z_lo, y, core), date: 16 (over z_hi, x).
Axes of the slice: x: 4, y: 4, z: 16 (z_hi: 4, z_lo: 4; z = z_hi * 4 + z_lo), core: 2. Of those that a mesh axis runs over, the one named last changes fastest.
Arguments:
- secondary: bfloat16 [16, 2, 3072, 1024], P('date', None, 'tile'), may hold values from -6 to 6
- primary: bfloat16 [2, 3072, 1024], P(None, 'tile', 'date'), may hold values from -6 to 6
- margin_mask: int32 [3072], P('tile'), may hold values from 0 to 1, as said below
- az_off: int32 [16, 32], P('date', 'tile'), may hold values from -16 to 16
- rg_off: int32 [16, 32], P('date', 'tile'), may hold values from -16 to 16
- az_frac: float32 [16, 32], P('date', 'tile'), may hold values from 0 to 1
- rg_frac: float32 [16, 32], P('date', 'tile'), may hold values from 0 to 1
Outputs:
- looks: float32 [16, 2, 1536, 128], P('date', None, 'tile')
Inputs may be any that keep to these rules, and one draw needn't show every extreme that they name: `margin_mask`: ones lie only in the last 64 rows of each tile of 96 rows, and the last row of every tile is 1.
All inputs are finite; a program needn't handle non-finite values.
Results may differ from a plain program's by a relative error of at most 0.017.
Values may be sent and summed in bfloat16 or wider, within the bound.
A program may use at most 64 MiB of HBM per device.

v0:
```python
import jax
import jax.numpy as jnp
from jax import lax
from jax.sharding import PartitionSpec as P

KA = 16
LAG = 64
LA = 2
LR = 8


def padded(block, sides, width):
    for axis, dim in sides:
        count = lax.axis_size(axis)
        forward = [(i, i + 1) for i in range(count - 1)]
        backward = [(target, source) for source, target in forward]
        low = lax.ppermute(
            lax.slice_in_dim(block, block.shape[dim] - width, None, axis=dim), axis, forward
        )
        high = lax.ppermute(lax.slice_in_dim(block, 0, width, axis=dim), axis, backward)
        block = jnp.concatenate([low, block, high], axis=dim)
    return block


def passed_along(value, axis, steps):
    count = lax.axis_size(axis)
    initial, last = (max(0, -steps), min(count, count - steps))
    return lax.ppermute(value, axis, [(source, source + steps) for source in range(initial, last)])


def window(dist):
    return jnp.sinc(dist) * (0.5 + 0.5 * jnp.cos(jnp.pi * dist / 4.0))


def band_taps(offset, frac):
    inside = (offset >= -3) & (offset <= 4)
    return jnp.where(inside, window(offset.astype(jnp.float32) - frac), 0.0).astype(jnp.bfloat16)


def multilook(values):
    depth, rows_n, cols_n = values.shape
    return values.reshape(depth, rows_n // LA, LA, cols_n // LR, LR).mean(axis=(2, 4))


def shards(secondary, primary, margin_mask, az_off, rg_off, az_frac, rg_frac):
    rim_rows = KA + 4
    block_cols = 256
    image = secondary[0]
    rows_n = image.shape[1]
    cols_n = image.shape[2]
    extended = padded(image, (("tile", 1),), rim_rows)
    row_out = lax.broadcasted_iota(jnp.int32, (rows_n, rows_n + 2 * rim_rows), 0)
    row_in = lax.broadcasted_iota(jnp.int32, (rows_n, rows_n + 2 * rim_rows), 1)
    azim_taps = band_taps(row_in - row_out - az_off[0, 0] - rim_rows, az_frac[0, 0])
    azim = jnp.einsum(
        "im,kmc->kic", azim_taps, extended, preferred_element_type=jnp.float32
    ).astype(jnp.bfloat16)
    blocks_n = cols_n // block_cols
    col_pad = jnp.pad(azim, ((0, 0), (0, 0), (block_cols // 2, block_cols // 2)))
    pieces = col_pad.reshape(2, rows_n, blocks_n + 1, block_cols)
    inputs = jnp.concatenate([pieces[:, :, :-1], pieces[:, :, 1:]], axis=3)
    col_in = lax.broadcasted_iota(jnp.int32, (2 * block_cols, block_cols), 0)
    col_out = lax.broadcasted_iota(jnp.int32, (2 * block_cols, block_cols), 1)
    range_taps = band_taps(col_in - block_cols // 2 - col_out - rg_off[0, 0], rg_frac[0, 0])
    resampled = jnp.einsum("kibm,mn->kibn", inputs, range_taps, preferred_element_type=jnp.float32)
    resampled = resampled.reshape(2, rows_n, cols_n).astype(jnp.bfloat16)
    prim = lax.all_gather(primary, "date", axis=2, tiled=True)[None]
    moved = resampled[None]
    sec_f = moved.astype(jnp.float32)
    prim_f = prim.astype(jnp.float32)
    ifg_re = prim_f[:, 0] * sec_f[:, 0] + prim_f[:, 1] * sec_f[:, 1]
    ifg_im = prim_f[:, 1] * sec_f[:, 0] - prim_f[:, 0] * sec_f[:, 1]
    interf = jnp.stack((ifg_re, ifg_im), axis=1)
    upcoming = passed_along(interf[:, :, :LAG, :], "tile", -1)
    later = jnp.concatenate([interf[:, :, LAG:, :], upcoming], axis=2)
    l_re = later[:, 0]
    l_im = later[:, 1]
    weight = margin_mask.astype(jnp.float32)[None, :, None]
    e_re = jnp.sum(weight * (ifg_re * l_re + ifg_im * l_im), axis=(1, 2))
    e_im = jnp.sum(weight * (ifg_im * l_re - ifg_re * l_im), axis=(1, 2))
    power = jnp.sum(
        weight * 0.5 * (ifg_re * ifg_re + ifg_im * ifg_im + l_re * l_re + l_im * l_im), axis=(1, 2)
    )
    count = jnp.zeros_like(e_re) + jnp.sum(margin_mask.astype(jnp.float32)) * interf.shape[3]
    stats = jnp.stack((e_re, e_im, power, count), axis=1)
    totals = lax.psum(stats, "tile")
    magnitude = jnp.sqrt(totals[:, 0] * totals[:, 0] + totals[:, 1] * totals[:, 1])
    floor_val = (totals[:, 2] + 1e-06) / jnp.sqrt(jnp.maximum(totals[:, 3], 1.0))
    denom = jnp.maximum(magnitude, floor_val)
    u_re = (totals[:, 0] / denom)[:, None, None]
    u_im = (totals[:, 1] / denom)[:, None, None]
    c_re = multilook(ifg_re * u_re + ifg_im * u_im)
    c_im = multilook(ifg_im * u_re - ifg_re * u_im)
    result = jnp.stack((c_re, c_im), axis=1)
    return result


def solution(mesh):
    return jax.shard_map(
        shards,
        mesh=mesh,
        in_specs=(
            P("date", None, "tile", None),
            P(None, "tile", "date"),
            P("tile"),
            P("date", "tile"),
            P("date", "tile"),
            P("date", "tile"),
            P("date", "tile"),
        ),
        out_specs=P("date", None, "tile", None),
        check_vma=False,
    )
```

profile of v0, /device:TPU:1, one launch (start us, length us, event | category | flops | bytes accessed | tf_op | source)
XLA Modules:
  0.0 181.6 jit_solution(2312911935924852726)
XLA Ops:
  0.0 0.0 copy-start
  0.0 1.0 fusion.116
  1.0 4.6 %collective-permute-start = (bf16[2,20,1024]{2,1,0:T(8,128)(2,1)S(1)}, bf16[2,20,1024]{2,1,0:T(8,128)(2,1)S(1)}, u32[]{:S(2)}, u32[]{:S(2)}) collective-permute-start(bf16[2,20,1024]{2,1,0:T(8,128)(2,1)S(1)} %get-tuple-element.14), channel_id=1, source_target_pairs={{0,16},{16,32},{32,48},{48,64},{64,80},{80,96},{96,112},{112,128},... | collective-permute-start | bytes 245768 | tf_op jit(solution)/shard_map/ppermute | solution.py:17
  5.6 5.5 %collective-permute-start.1 = (bf16[2,20,1024]{2,1,0:T(8,128)(2,1)S(1)}, bf16[2,20,1024]{2,1,0:T(8,128)(2,1)S(1)}, u32[]{:S(2)}, u32[]{:S(2)}) collective-permute-start(bf16[2,20,1024]{2,1,0:T(8,128)(2,1)S(1)} %get-tuple-element.15), channel_id=1, source_target_pairs={{16,0},{32,16},{48,32},{64,48},{80,64},{96,80},{112,96},{128,112},... | collective-permute-start | bytes 245768 | tf_op jit(solution)/shard_map/ppermute | solution.py:20
  13.7 0.8 copy.15
  14.5 55.4 %all_gather.3 = bf16[2,96,1024]{1,0,2:T(2,128)(2,1)S(1)} all-gather(bf16[2,96,64]{1,0,2:T(2,128)(2,1)S(1)} %copy.15), channel_id=1, replica_groups=mesh['tile'=32,'date'=16] {'date'}, dimensions={2}, use_global_device_ids=true | all-gather | bytes 417792 | tf_op jit(solution)/shard_map/all_gather | solution.py:67
  69.9 0.4 copy.16
  70.3 0.1 bitcast_convert_fusion
  70.4 0.0 collective-permute-done
  70.4 0.0 collective-permute-done.1
  70.4 0.0 copy-done
  70.4 0.6 fusion.1
  71.1 0.3 copy.24
  71.3 0.1 pad.4.clone
  71.5 0.2 fusion.115
  71.7 0.2 copy.22
  71.9 0.2 copy.23
  72.1 2.9 %fusion = f32[2,96,4,256]{3,1,2,0:T(8,128)S(1)} fusion(bf16[2,96,4,256]{3,1,2,0:T(8,128)(2,1)S(1)} %copy.23, bf16[2,96,4,256]{3,1,2,0:T(8,128)(2,1)S(1)} %copy.22, f32[]{:T(128)} %bitcast.51, s32[]{:T(128)} %bitcast.49, s32[512]{0:T(512)S(1)} %iota_add_fusion), kind=kOutput, calls=%fused_computation.2 | convolution fusion | flops 209321984 | bytes 1574920 | tf_op jit(solution)/shard_map/kibm,mn->kibn/dot_general | solution.py:65
  75.0 0.5 copy.20
  75.5 0.4 reshape.581
  75.9 0.0 copy-start.1
  75.9 0.2 multiply_subtract_fusion.1
  76.1 3.9 %collective-permute-start.2 = (f32[1,2,64,1024]{3,2,1,0:T(8,128)S(1)}, f32[1,2,64,1024]{3,2,1,0:T(8,128)S(1)}, u32[]{:S(2)}, u32[]{:S(2)}) collective-permute-start(f32[1,2,64,1024]{3,2,1,0:T(8,128)S(1)} %pad_maximum_fusion.1), channel_id=1, source_target_pairs={{16,0},{32,16},{48,32},{64,48},{80,64},{96,80},{112,96},{128,112},... | collective-permute-start | bytes 1572872 | tf_op jit(solution)/shard_map/ppermute | solution.py:28
  80.0 0.0 copy-done.1
  80.0 0.6 broadcast_multiply_fusion
  81.3 12.3 %collective-permute-done.2 = f32[1,2,64,1024]{3,2,1,0:T(8,128)S(1)} collective-permute-done((f32[1,2,64,1024]{3,2,1,0:T(8,128)S(1)}, f32[1,2,64,1024]{3,2,1,0:T(8,128)S(1)}, u32[]{:S(2)}, u32[]{:S(2)}) %collective-permute-start.2) | collective-permute-done | bytes 524320 | tf_op jit(solution)/shard_map/ppermute | solution.py:28
  93.6 0.1 fusion.2
  93.7 1.0 fusion.29
  94.7 2.0 %pad_maximum_fusion.3 = f32[1,4]{1,0:T(1,128)S(1)} fusion(f32[1,1]{1,0:T(1,128)} %bitcast.18, f32[1,1]{1,0:T(1,128)} %bitcast.17, f32[1,1]{1,0:T(1,128)} %bitcast.15, f32[1,1]{1,0:T(1,128)} %bitcast.13), kind=kLoop, calls=%fused_computation.124 | loop fusion | flops 12 | bytes 32 | tf_op jit(solution)/shard_map/stack | solution.py:85
  96.6 61.0 %psum.7 = f32[1,4]{1,0:T(1,128)S(1)} all-reduce(f32[1,4]{1,0:T(1,128)S(1)} %pad_maximum_fusion.3), channel_id=1, replica_groups=mesh['tile'=32,'date'=16] {'tile'}, use_global_device_ids=true, to_apply=%region_4.5 | all-reduce | flops 4 | bytes 32 | tf_op jit(solution)/shard_map/psum | solution.py:86
  157.7 0.6 fusion.117
  163.6 0.1 multiply_add_fusion.1
  163.7 5.0 %add.275 = f32[48,2,128,8]{3,2,1,0:T(8,128)} reshape(f32[1,1,96,1024]{3,2,1,0:T(8,128)S(1)} %get-tuple-element.10) | data formatting | bytes 786432 | tf_op jit(solution)/shard_map/add | solution.py:92
  168.6 5.0 %sub.152 = f32[48,2,128,8]{3,2,1,0:T(8,128)} reshape(f32[1,1,96,1024]{3,2,1,0:T(8,128)S(1)} %get-tuple-element.11) | data formatting | bytes 786432 | tf_op jit(solution)/shard_map/sub | solution.py:93
  173.6 3.7 %reduce_sum.58 = f32[48,128]{1,0:T(8,128)S(1)} reduce(f32[48,2,128,8]{3,2,1,0:T(8,128)} %add.275, f32[]{:T(128)} %constant.55.clone.1), dimensions={1,3}, to_apply=%region_5.6 | reduce | flops 92160 | bytes 417796 | tf_op jit(solution)/shard_map/reduce_sum | solution.py:42
  177.3 3.7 %reduce_sum.59 = f32[48,128]{1,0:T(8,128)S(1)} reduce(f32[48,2,128,8]{3,2,1,0:T(8,128)} %sub.152, f32[]{:T(128)} %constant.55.clone.1), dimensions={1,3}, to_apply=%region_6.7 | reduce | flops 92160 | bytes 417796 | tf_op jit(solution)/shard_map/reduce_sum | solution.py:42
  181.0 0.6 pad_maximum_fusion.2
  (4 shorter events, 0.1 us)
Async XLA Ops:
  0.0 70.4 %copy-start = (bf16[1,2,96,1024]{3,2,1,0:T(8,128)(2,1)S(1)}, bf16[1,2,96,1024]{3,2,1,0:T(8,128)(2,1)}, u32[]{:S(2)}) copy-start(bf16[1,2,96,1024]{3,2,1,0:T(8,128)(2,1)} %param.7) | copy-start | bytes 1179652
  1.0 69.4 %collective-permute-start = (bf16[2,20,1024]{2,1,0:T(8,128)(2,1)S(1)}, bf16[2,20,1024]{2,1,0:T(8,128)(2,1)S(1)}, u32[]{:S(2)}, u32[]{:S(2)}) collective-permute-start(bf16[2,20,1024]{2,1,0:T(8,128)(2,1)S(1)} %get-tuple-element.14), channel_id=1, source_target_pairs={{0,16},{16,32},{32,48},{48,64},{64,80},{80,96},{96,112},{112,128},... | collective-permute-start | bytes 245768 | tf_op jit(solution)/shard_map/ppermute | solution.py:17
  5.6 64.8 %collective-permute-start.1 = (bf16[2,20,1024]{2,1,0:T(8,128)(2,1)S(1)}, bf16[2,20,1024]{2,1,0:T(8,128)(2,1)S(1)}, u32[]{:S(2)}, u32[]{:S(2)}) collective-permute-start(bf16[2,20,1024]{2,1,0:T(8,128)(2,1)S(1)} %get-tuple-element.15), channel_id=1, source_target_pairs={{16,0},{32,16},{48,32},{64,48},{80,64},{96,80},{112,96},{128,112},... | collective-permute-start | bytes 245768 | tf_op jit(solution)/shard_map/ppermute | solution.py:20
  75.9 4.1 %copy-start.1 = (s32[96]{0:T(128)S(1)}, s32[96]{0:T(128)}, u32[]{:S(2)}) copy-start(s32[96]{0:T(128)} %param.9) | copy-start | bytes 1156
  76.1 17.5 %collective-permute-start.2 = (f32[1,2,64,1024]{3,2,1,0:T(8,128)S(1)}, f32[1,2,64,1024]{3,2,1,0:T(8,128)S(1)}, u32[]{:S(2)}, u32[]{:S(2)}) collective-permute-start(f32[1,2,64,1024]{3,2,1,0:T(8,128)S(1)} %pad_maximum_fusion.1), channel_id=1, source_target_pairs={{16,0},{32,16},{48,32},{64,48},{80,64},{96,80},{112,96},{128,112},... | collective-permute-start | bytes 1572872 | tf_op jit(solution)/shard_map/ppermute | solution.py:28
where the time goes:
time: 182 us
  blocking collectives  116 us (64%)
  local copies, waits for them, and re-layouts  14.7 us (8%)
  starting transfers between devices  13.9 us (8%)
  waiting for transfers between devices  12.3 us (7%)
  other arithmetic  12 us (7%)
  between operations  8.73 us (5%)
  matrix products  3.52 us (2%)
    psum x1, blocking collectives, shards(): totals = lax.psum(stats, 'tile')  61 us
    all_gather x1, blocking collectives, shards(): prim = lax.all_gather(primary, 'date', axis=2, tiled=True)[None]  55.4 us
    ppermute x1, waiting for transfers between devices, passed_along(): lax.ppermute(value, axis, [(source, source + steps) for source in range(i...  12.3 us
    reduce_sum x2, other arithmetic, multilook(): values.reshape(depth, rows_n // LA, LA, cols_n // LR, LR).mean(axis=(2, 4))  7.34 us
    ppermute x1, starting transfers between devices, padded(): lax.ppermute(lax.slice_in_dim(block, 0, width, axis=dim), axis, backward)  5.46 us
    sub x1, local copies, waits for them, and re-layouts, shards(): c_im = multilook(ifg_im * u_re - ifg_re * u_im)  4.97 us
    add x1, local copies, waits for them, and re-layouts, shards(): c_re = multilook(ifg_re * u_re + ifg_im * u_im)  4.95 us
    ppermute x1, starting transfers between devices, padded(): lax.ppermute(lax.slice_in_dim(block, block.shape[dim] - width, None, axis...  4.58 us
  transfers between devices with their start and end apart: 3, of which 1 were waited for; matrix products, arithmetic and copies ran while one was open for 1% of the time, Pallas kernels for 0%

commit v1 on v0

--- a/solution.py
+++ b/solution.py
@@ -7,6 +7,13 @@
 LAG = 64
 LA = 2
 LR = 8
+
+
+def swapped_in(x, name, dim):
+    peers = lax.axis_size(name)
+    pieces = jnp.stack([x for _ in range(peers)])
+    pieces = lax.all_to_all(pieces, name, split_axis=0, concat_axis=0)
+    return jnp.concatenate(pieces, axis=dim)
 
 
 def padded(block, sides, width):
@@ -64,7 +71,7 @@
     range_taps = band_taps(col_in - block_cols // 2 - col_out - rg_off[0, 0], rg_frac[0, 0])
     resampled = jnp.einsum("kibm,mn->kibn", inputs, range_taps, preferred_element_type=jnp.float32)
     resampled = resampled.reshape(2, rows_n, cols_n).astype(jnp.bfloat16)
-    prim = lax.all_gather(primary, "date", axis=2, tiled=True)[None]
+    prim = swapped_in(primary, "date", 2)[None]
     moved = resampled[None]
     sec_f = moved.astype(jnp.float32)
     prim_f = prim.astype(jnp.float32)

time: 182 us -> 155 us (0.85)
  blocking collectives: 116 us -> 64.6 us
  starting transfers between devices: 13.9 us -> 36 us
    all_gather x1 -> x0, blocking collectives: 55.4 us -> none  [shards(): prim = lax.all_gather(primary, 'date', axis=2, tiled=True)[None]]
    all_to_all x0 -> x1, starting transfers between devices: none -> 18.2 us  [swapped_in(): pieces = lax.all_to_all(pieces, name, split_axis=0, concat_axis=0)]
    ppermute x1, starting transfers between devices: 3.89 us -> 11.9 us  [passed_along(): lax.ppermute(value, axis, [(source, source + steps) for source in range(i...]
    ppermute x1, waiting for transfers between devices: 12.3 us -> 6.4 us  [passed_along(): lax.ppermute(value, axis, [(source, source + steps) for source in range(i...]
    all_to_all x0 -> x1, waiting for transfers between devices: none -> 4.76 us  [swapped_in(): pieces = lax.all_to_all(pieces, name, split_axis=0, concat_axis=0)]
    ppermute x1, starting transfers between devices: 5.46 us -> 1.92 us  [padded(): lax.ppermute(lax.slice_in_dim(block, 0, width, axis=dim), axis, backward)]
    psum x1, blocking collectives: 61 us -> 64.6 us  [shards(): totals = lax.psum(stats, 'tile')]
    sub x1 -> x2, local copies, waits for them, and re-layouts: 4.97 us -> 5.18 us  [shards(): c_im = multilook(ifg_im * u_re - ifg_re * u_im)]
  transfers between devices with their start and end apart: 3 -> 4, of which waited for: 1 -> 3; matrix products, arithmetic and copies ran while one was open for 1% -> 4% of each run, Pallas kernels for 0% -> 0%
where the time goes in v1:
time: 155 us; the launch traced here: 154 us
  blocking collectives  64.6 us (42%)
  starting transfers between devices  36 us (23%)
  local copies, waits for them, and re-layouts  15.7 us (10%)
  other arithmetic  12.6 us (8%)
  waiting for transfers between devices  12.6 us (8%)
  between operations  8.75 us (6%)
  matrix products  3.52 us (2%)
    psum x1, blocking collectives, shards(): totals = lax.psum(stats, 'tile')  64.6 us
    all_to_all x1, starting transfers between devices, swapped_in(): pieces = lax.all_to_all(pieces, name, split_axis=0, concat_axis=0)  18.2 us
    ppermute x1, starting transfers between devices, passed_along(): lax.ppermute(value, axis, [(source, source + steps) for source in range(i...  11.9 us
    reduce_sum x2, other arithmetic, multilook(): values.reshape(depth, rows_n // LA, LA, cols_n // LR, LR).mean(axis=(2, 4))  7.34 us
    ppermute x1, waiting for transfers between devices, passed_along(): lax.ppermute(value, axis, [(source, source + steps) for source in range(i...  6.4 us
    sub x2, local copies, waits for them, and re-layouts, shards(): c_im = multilook(ifg_im * u_re - ifg_re * u_im)  5.18 us
    add x2, local copies, waits for them, and re-layouts, shards(): c_re = multilook(ifg_re * u_re + ifg_im * u_im)  5.12 us
    all_to_all x1, waiting for transfers between devices, swapped_in(): pieces = lax.all_to_all(pieces, name, split_axis=0, concat_axis=0)  4.76 us
  transfers between devices with their start and end apart: 4, of which 3 were waited for; matrix products, arithmetic and copies ran while one was open for 4% of the time, Pallas kernels for 0%

profile of v1, /device:TPU:1, one launch (start us, length us, event | category | flops | bytes accessed | tf_op | source)
XLA Modules:
  0.0 153.7 jit_solution(3965809137271125351)
XLA Ops:
  0.0 0.0 copy-start
  0.0 1.7 %stack.14 = bf16[16,2,96,64]{2,3,1,0:T(8,128)(2,1)} broadcast(bf16[2,96,64]{1,2,0:T(8,128)(2,1)} %param.8), dimensions={1,2,3} | broadcast | bytes 417792 | tf_op jit(solution)/shard_map/stack | solution.py:14
  1.7 18.2 %all-to-all-start = ((bf16[16,2,96,64]{2,3,1,0:T(8,128)(2,1)}), bf16[16,2,96,64]{2,3,1,0:T(8,128)(2,1)S(1)}, u32[]{:S(2)}, u32[]{:S(2)}) async-start(bf16[16,2,96,64]{2,3,1,0:T(8,128)(2,1)} %stack.14), calls=%async_computation | async-start | bytes 1048576 | tf_op jit(solution)/shard_map/all_to_all | solution.py:15
  19.9 0.0 copy-done
  20.0 4.0 %collective-permute-start = (bf16[2,20,1024]{2,1,0:T(8,128)(2,1)S(1)}, bf16[2,20,1024]{2,1,0:T(8,128)(2,1)S(1)}, u32[]{:S(2)}, u32[]{:S(2)}) collective-permute-start(bf16[2,20,1024]{2,1,0:T(8,128)(2,1)S(1)} %get-tuple-element.14), channel_id=1, source_target_pairs={{0,16},{16,32},{32,48},{48,64},{64,80},{80,96},{96,112},{112,128},... | collective-permute-start | bytes 245768 | tf_op jit(solution)/shard_map/ppermute | solution.py:24
  24.0 1.9 %collective-permute-start.1 = (bf16[2,20,1024]{2,1,0:T(8,128)(2,1)S(1)}, bf16[2,20,1024]{2,1,0:T(8,128)(2,1)S(1)}, u32[]{:S(2)}, u32[]{:S(2)}) collective-permute-start(bf16[2,20,1024]{2,1,0:T(8,128)(2,1)S(1)} %get-tuple-element.15), channel_id=1, source_target_pairs={{16,0},{32,16},{48,32},{64,48},{80,64},{96,80},{112,96},{128,112},... | collective-permute-start | bytes 245768 | tf_op jit(solution)/shard_map/ppermute | solution.py:27
  28.5 0.0 collective-permute-done
  28.6 1.4 collective-permute-done.1
  30.0 0.6 fusion.1
  30.6 0.3 copy.35
  30.9 0.1 pad.4.clone
  31.0 0.2 fusion.115
  31.2 0.2 copy.33
  31.4 0.2 copy.34
  31.6 2.9 %fusion = f32[2,96,4,256]{3,1,2,0:T(8,128)S(1)} fusion(bf16[2,96,4,256]{3,1,2,0:T(8,128)(2,1)S(1)} %copy.34, bf16[2,96,4,256]{3,1,2,0:T(8,128)(2,1)S(1)} %copy.33, f32[]{:T(128)} %bitcast.52, s32[]{:T(128)} %bitcast.50, s32[512]{0:T(512)S(1)} %iota_add_fusion), kind=kOutput, calls=%fused_computation.2 | convolution fusion | flops 209321984 | bytes 1574920 | tf_op jit(solution)/shard_map/kibm,mn->kibn/dot_general | solution.py:72
  34.5 0.3 copy.31
  34.8 4.8 %all-to-all-done = bf16[16,2,96,64]{2,3,1,0:T(8,128)(2,1)S(1)} async-done(((bf16[16,2,96,64]{2,3,1,0:T(8,128)(2,1)}), bf16[16,2,96,64]{2,3,1,0:T(8,128)(2,1)S(1)}, u32[]{:S(2)}, u32[]{:S(2)}) %all-to-all-start) | async-done | bytes 393248 | tf_op jit(solution)/shard_map/all_to_all | solution.py:15
  39.6 0.1 convert_bitcast_fusion
  39.7 0.1 copy.19
  39.8 0.1 multiply_subtract_fusion.1
  39.9 0.0 copy-start.1
  39.9 0.1 pad_maximum_fusion
  40.0 0.3 copy.26
  40.3 11.9 %collective-permute-start.2 = (f32[1,2,64,1024]{3,2,1,0:T(8,128)S(1)}, f32[1,2,64,1024]{3,2,1,0:T(8,128)}, u32[]{:S(2)}, u32[]{:S(2)}) collective-permute-start(f32[1,2,64,1024]{3,2,1,0:T(8,128)S(1)} %copy.26), channel_id=1, source_target_pairs={{16,0},{32,16},{48,32},{64,48},{80,64},{96,80},{112,96},{128,112},... | collective-permute-start | bytes 1572872 | tf_op jit(solution)/shard_map/ppermute | solution.py:35
  52.2 0.0 copy-done.1
  52.2 0.6 broadcast_multiply_fusion
  53.5 0.3 slice_maximum_fusion
  53.8 6.4 %collective-permute-done.2 = f32[1,2,64,1024]{3,2,1,0:T(8,128)} collective-permute-done((f32[1,2,64,1024]{3,2,1,0:T(8,128)S(1)}, f32[1,2,64,1024]{3,2,1,0:T(8,128)}, u32[]{:S(2)}, u32[]{:S(2)}) %collective-permute-start.2) | collective-permute-done | bytes 524320 | tf_op jit(solution)/shard_map/ppermute | solution.py:35
  60.2 1.4 copy.27
  61.6 1.3 fusion.21
  62.9 2.0 %pad_maximum_fusion.3 = f32[1,4]{1,0:T(1,128)S(1)} fusion(f32[1,1]{1,0:T(1,128)} %bitcast.18, f32[1,1]{1,0:T(1,128)} %bitcast.17, f32[1,1]{1,0:T(1,128)} %bitcast.15, f32[1,1]{1,0:T(1,128)} %bitcast.13), kind=kLoop, calls=%fused_computation.127 | loop fusion | flops 12 | bytes 32 | tf_op jit(solution)/shard_map/stack | solution.py:92
  64.8 64.6 %psum.7 = f32[1,4]{1,0:T(1,128)S(1)} all-reduce(f32[1,4]{1,0:T(1,128)S(1)} %pad_maximum_fusion.3), channel_id=1, replica_groups=mesh['tile'=32,'date'=16] {'tile'}, use_global_device_ids=true, to_apply=%region_4.5 | all-reduce | flops 4 | bytes 32 | tf_op jit(solution)/shard_map/psum | solution.py:93
  129.4 0.6 fusion.117
  135.3 0.1 multiply_add_fusion.1
  135.4 0.2 copy.28
  135.6 0.2 copy.29
  135.8 5.0 %sub.152 = f32[48,2,128,8]{3,2,1,0:T(8,128)} reshape(f32[1,1,96,1024]{3,2,1,0:T(8,128)S(1)} %copy.29) | data formatting | bytes 786432 | tf_op jit(solution)/shard_map/sub | solution.py:100
  140.8 4.9 %add.275 = f32[48,2,128,8]{3,2,1,0:T(8,128)} reshape(f32[1,1,96,1024]{3,2,1,0:T(8,128)S(1)} %copy.28) | data formatting | bytes 786432 | tf_op jit(solution)/shard_map/add | solution.py:99
  145.8 3.7 %reduce_sum.59 = f32[48,128]{1,0:T(8,128)S(1)} reduce(f32[48,2,128,8]{3,2,1,0:T(8,128)} %sub.152, f32[]{:T(128)} %constant.55.clone.1), dimensions={1,3}, to_apply=%region_6.7 | reduce | flops 92160 | bytes 417796 | tf_op jit(solution)/shard_map/reduce_sum | solution.py:49
  149.4 3.7 %reduce_sum.58 = f32[48,128]{1,0:T(8,128)S(1)} reduce(f32[48,2,128,8]{3,2,1,0:T(8,128)} %add.275, f32[]{:T(128)} %constant.55.clone.1), dimensions={1,3}, to_apply=%region_5.6 | reduce | flops 92160 | bytes 417796 | tf_op jit(solution)/shard_map/reduce_sum | solution.py:49
  153.1 0.6 pad_maximum_fusion.2
  (4 shorter events, 0.0 us)
Async XLA Ops:
  0.0 19.9 %copy-start = (bf16[1,2,96,1024]{3,2,1,0:T(8,128)(2,1)S(1)}, bf16[1,2,96,1024]{3,2,1,0:T(8,128)(2,1)}, u32[]{:S(2)}) copy-start(bf16[1,2,96,1024]{3,2,1,0:T(8,128)(2,1)} %param.7) | copy-start | bytes 1179652
  1.7 37.9 %all-to-all-start = ((bf16[16,2,96,64]{2,3,1,0:T(8,128)(2,1)}), bf16[16,2,96,64]{2,3,1,0:T(8,128)(2,1)S(1)}, u32[]{:S(2)}, u32[]{:S(2)}) async-start(bf16[16,2,96,64]{2,3,1,0:T(8,128)(2,1)} %stack.14), calls=%async_computation | async-start | bytes 1048576 | tf_op jit(solution)/shard_map/all_to_all | solution.py:15
  20.0 8.6 %collective-permute-start = (bf16[2,20,1024]{2,1,0:T(8,128)(2,1)S(1)}, bf16[2,20,1024]{2,1,0:T(8,128)(2,1)S(1)}, u32[]{:S(2)}, u32[]{:S(2)}) collective-permute-start(bf16[2,20,1024]{2,1,0:T(8,128)(2,1)S(1)} %get-tuple-element.14), channel_id=1, source_target_pairs={{0,16},{16,32},{32,48},{48,64},{64,80},{80,96},{96,112},{112,128},... | collective-permute-start | bytes 245768 | tf_op jit(solution)/shard_map/ppermute | solution.py:24
  24.0 5.9 %collective-permute-start.1 = (bf16[2,20,1024]{2,1,0:T(8,128)(2,1)S(1)}, bf16[2,20,1024]{2,1,0:T(8,128)(2,1)S(1)}, u32[]{:S(2)}, u32[]{:S(2)}) collective-permute-start(bf16[2,20,1024]{2,1,0:T(8,128)(2,1)S(1)} %get-tuple-element.15), channel_id=1, source_target_pairs={{16,0},{32,16},{48,32},{64,48},{80,64},{96,80},{112,96},{128,112},... | collective-permute-start | bytes 245768 | tf_op jit(solution)/shard_map/ppermute | solution.py:27
  39.9 12.3 %copy-start.1 = (s32[96]{0:T(128)S(1)}, s32[96]{0:T(128)}, u32[]{:S(2)}) copy-start(s32[96]{0:T(128)} %param.9) | copy-start | bytes 1156
  40.3 19.9 %collective-permute-start.2 = (f32[1,2,64,1024]{3,2,1,0:T(8,128)S(1)}, f32[1,2,64,1024]{3,2,1,0:T(8,128)}, u32[]{:S(2)}, u32[]{:S(2)}) collective-permute-start(f32[1,2,64,1024]{3,2,1,0:T(8,128)S(1)} %copy.26), channel_id=1, source_target_pairs={{16,0},{32,16},{48,32},{64,48},{80,64},{96,80},{112,96},{128,112},... | collective-permute-start | bytes 1572872 | tf_op jit(solution)/shard_map/ppermute | solution.py:35
